TPU v7x, 32 devices: a whole 2x2x4 slice. The times are simulated.
32 devices in a mesh: ops: 16 (over z, y, core), sec: 2 (over x).
Axes of the slice: x: 2, y: 2, z: 4, core: 2. Of those that a mesh axis runs over, the one named last changes fastest.
Arguments:
- wavefunction: bfloat16 [2, 512, 512], P('sec', 'ops'), may hold values from -6 to 6
- left_blocks: bfloat16 [2, 64, 512, 512], P('sec', 'ops'), may hold values from -0.25 to 0.25
- right_blocks: bfloat16 [2, 64, 512, 512], P('sec', 'ops'), may hold values from -0.0625 to 0.0625
- pair_index: int32 [2, 64], P('sec', 'ops'), may hold values from 0 to 3
- term_counts: int32 [2, 16], P('sec'), may hold values from 0 to 4, as said below
- charges: int32 [2], P('sec'), may hold values from 0 to 7
Outputs:
- applied: bfloat16 [2, 512, 512], P('sec', 'ops')
Inputs may be any that keep to these rules, and one draw needn't show every extreme that they name: `term_counts`: in every sector exactly one device row holds 4 live terms and every other holds 0 to 2; live terms fill a device's slots from slot 0 on.
All inputs are finite; a program needn't handle non-finite values.
Results may differ from a plain program's by a relative error of at most 0.0029.
Values may be sent and summed in bfloat16 or wider, within the bound.
A program may use at most 64 MiB of HBM per device.

v0:
```python
import jax
import jax.numpy as jnp
from jax import lax
from jax.sharding import PartitionSpec as P


def from_behind(x, axis, by):
    length = lax.axis_size(axis)
    pairs = [(i, i + by) for i in range(length) if 0 <= i + by < length]
    return lax.ppermute(x, axis, pairs)


def add_terms(running, gathered, left_slots, rights, pair_picks, live_count):

    def add_term(slot_index, current):
        left_rows = left_slots[slot_index]
        right_block = rights[pair_picks[slot_index]]
        product = jnp.dot(left_rows, gathered, preferred_element_type=jnp.float32).astype(
            jnp.bfloat16
        )
        return current + jnp.dot(product, right_block, preferred_element_type=jnp.float32)

    return lax.fori_loop(0, live_count, add_term, running)


def per_device(wavefunction, left_blocks, right_blocks, pair_index, term_counts, charges):
    own_rows = wavefunction[0]
    gathered = lax.all_gather(own_rows, "ops", axis=0, tiled=True)
    left_slots = left_blocks[0]
    rights = right_blocks[0]
    pair_picks = pair_index[0]
    columns = gathered.shape[1]
    position = lax.axis_index("ops")
    counts_row = term_counts[0]
    live_count = counts_row[position]
    band_rows = own_rows.shape[0]
    running = jnp.zeros((band_rows * lax.axis_size("ops"), columns), jnp.float32)
    summed = lax.psum_scatter(
        add_terms(running, gathered, left_slots, rights, pair_picks, live_count),
        "ops",
        scatter_dimension=0,
        tiled=True,
    )
    raised = from_behind(summed, "sec", 1)
    onsite = 0.5 * charges[0].astype(jnp.float32) * own_rows.astype(jnp.float32)
    return (onsite + raised).astype(jnp.bfloat16)[None]


def solution(mesh):
    return jax.shard_map(
        per_device,
        mesh=mesh,
        in_specs=(
            P("sec", "ops", None),
            P("sec", "ops", None, None),
            P("sec", "ops", None, None),
            P("sec", "ops"),
            P("sec", None),
            P("sec"),
        ),
        out_specs=P("sec", "ops", None),
        check_vma=False,
    )
```

profile of v0, /device:TPU:0, one launch (start us, length us, event | category | flops | bytes accessed | tf_op | source)
XLA Modules:
  0.0 122.8 jit_solution(15181813735898667096)
XLA Ops:
  6.5 0.0 copy-start
  6.5 0.0 reduce-scatter.2.cloned.1.call-start
  6.5 24.9 %all-gather = bf16[1,512,512]{2,1,0:T(8,128)(2,1)S(1)} all-gather(bf16[1,32,512]{2,1,0:T(8,128)(2,1)} %param.8), channel_id=2, replica_groups=mesh['ops'=16,'sec'=2] {'ops'}, dimensions={1}, use_global_device_ids=true | all-gather | bytes 557056 | tf_op jit(solution)/shard_map/all_gather | solution.py:28
  31.5 0.0 copy-done
  31.5 0.6 constant_dynamic-slice_fusion
  32.1 0.1 broadcast_in_dim.6
  32.2 0.0 copy-start.2
  32.2 0.6 while.10
  32.8 0.0 copy-start.1
  32.8 1.0 copy-done.1
  33.7 0.0 reduce-scatter.2.cloned.1.call-update
  33.8 75.9 %reduce-scatter.2.cloned.1.call-done = f32[32,512]{1,0:T(8,128)} async-done(((f32[512,512]{1,0:T(8,128)}), f32[32,512]{1,0:T(8,128)}) %reduce-scatter.2.cloned.1.call-update) | async-done | bytes 65552 | tf_op jit(solution)/shard_map/reduce_scatter | solution.py:38
  109.7 3.4 %collective-permute-start = (f32[32,512]{1,0:T(8,128)}, f32[32,512]{1,0:T(8,128)S(1)}, u32[]{:S(2)}, u32[]{:S(2)}) collective-permute-start(f32[32,512]{1,0:T(8,128)} %reduce-scatter.2.cloned.1.call-done), channel_id=1, source_target_pairs={{0,1},{2,3},{4,5},{6,7},{8,9},{10,11},{12,13},{14,15},{16,17},{18,... | collective-permute-start | bytes 196616 | tf_op jit(solution)/shard_map/ppermute | solution.py:10
  113.7 1.6 %collective-permute-done = f32[32,512]{1,0:T(8,128)S(1)} collective-permute-done((f32[32,512]{1,0:T(8,128)}, f32[32,512]{1,0:T(8,128)S(1)}, u32[]{:S(2)}, u32[]{:S(2)}) %collective-permute-start) | collective-permute-done | bytes 65568 | tf_op jit(solution)/shard_map/ppermute | solution.py:10
  115.3 0.0 copy-done.2
  115.3 0.6 fusion.9
Async XLA Ops:
  6.5 24.9 %copy-start = (s32[1,16]{1,0:T(1,128)S(1)}, s32[1,16]{1,0:T(1,128)}, u32[]{:S(2)}) copy-start(s32[1,16]{1,0:T(1,128)} %param.12) | copy-start | bytes 196
  6.5 103.1 %reduce-scatter.2.cloned.1.call-start = ((), (), s32[]{:S(2)}) async-start(), calls=%async_computation.1 | async-start | bytes 1114112 | tf_op jit(solution)/shard_map/reduce_scatter | solution.py:38
  32.2 83.1 %copy-start.2 = (bf16[1,32,512]{2,1,0:T(8,128)(2,1)S(1)}, bf16[1,32,512]{2,1,0:T(8,128)(2,1)}, u32[]{:S(2)}) copy-start(bf16[1,32,512]{2,1,0:T(8,128)(2,1)} %param.8) | copy-start | bytes 98308
  32.8 1.0 copy-start.1
  109.7 5.6 %collective-permute-start = (f32[32,512]{1,0:T(8,128)}, f32[32,512]{1,0:T(8,128)S(1)}, u32[]{:S(2)}, u32[]{:S(2)}) collective-permute-start(f32[32,512]{1,0:T(8,128)} %reduce-scatter.2.cloned.1.call-done), channel_id=1, source_target_pairs={{0,1},{2,3},{4,5},{6,7},{8,9},{10,11},{12,13},{14,15},{16,17},{18,... | collective-permute-start | bytes 196616 | tf_op jit(solution)/shard_map/ppermute | solution.py:10
Sparse Core Ops, SparseCore 0:
  33.9 75.7 reduce-scatter.1
where the time goes:
time: 124 us; the launch traced here: 123 us
  waiting for transfers between devices  77.5 us (62%)
  blocking collectives  24.9 us (20%)
  between operations  14.1 us (11%)
  starting transfers between devices  3.39 us (3%)
  local copies, waits for them, and re-layouts  1.67 us (1%)
    reduce_scatter x1, waiting for transfers between devices, per_device(): lax.psum_scatter(add_terms(running, gathered, left_slots, rights, pair_pi...  75.9 us
    all_gather x1, blocking collectives, per_device(): gathered = lax.all_gather(own_rows, 'ops', axis=0, tiled=True)  24.9 us
    ppermute x1, starting transfers between devices, from_behind(): return lax.ppermute(x, axis, pairs)  3.39 us
  transfers between devices with their start and end apart: 2, of which 2 were waited for; matrix products, arithmetic and copies ran while one was open for 0% of the time, Pallas kernels for 0%

commit v1 on v0

--- a/solution.py
+++ b/solution.py
@@ -1,7 +1,244 @@
+import functools
+
 import jax
 import jax.numpy as jnp
 from jax import lax
+from jax.experimental import pallas as pl
+from jax.experimental.pallas import tpu as pltpu
 from jax.sharding import PartitionSpec as P
+
+MESH = pl.DeviceIdType.MESH
+CORES = 2
+ROW_TILE = 16
+CHUNKS = 2
+
+
+def line_lengths(chips):
+    first = 1
+    while first * first < chips or chips % first:
+        first += 1
+    return first, chips // first
+
+
+def kernel(
+    lines, crosses, sectors,
+    picks_ref, counts_ref, charges_ref, own_hbm, left_hbm, right_hbm,
+    out_ref,
+    state, left, right, mine, theirs, banded, landed,
+    load_sem, line_send, line_recv, cross_send, cross_recv, core_send, core_recv,
+    half_send, half_recv, band_send, band_recv, ready_sem,
+):
+    position = lax.axis_index("ops")
+    sector = lax.axis_index("sec")
+    core = lax.rem(position, CORES)
+    chip = position // CORES
+    cross = lax.rem(chip, crosses)
+    line = chip // crosses
+    slots, chips, _, band, columns = left.shape
+    per_chunk = chips // CHUNKS
+    rows = per_chunk * band
+    last = sectors - 1
+
+    def index_of(a, b, c):
+        return (a * crosses + b) * CORES + c
+
+    def line_at(step):
+        return lax.rem(line + step, lines)
+
+    def cross_at(step):
+        return lax.rem(cross + step, crosses)
+
+    other = CORES - 1 - core
+
+    own_load = pltpu.make_async_copy(own_hbm, state.at[position], load_sem.at[0])
+    own_load.start()
+    left_load = pltpu.make_async_copy(left_hbm, left, load_sem.at[1])
+    right_load = pltpu.make_async_copy(right_hbm, right, load_sem.at[2])
+
+    barrier = pltpu.get_barrier_semaphore()
+    peers = [index_of(line_at(k), cross, core) for k in range(1, lines)]
+    peers += [index_of(line, cross_at(k), core) for k in range(1, crosses)]
+    peers += [index_of(line, cross, other)]
+    for peer in peers:
+        pl.semaphore_signal(barrier, inc=1, device_id={"ops": peer}, device_id_type=MESH)
+
+    @pl.when(sector > 0)
+    def _():
+        pl.semaphore_signal(barrier, inc=1, device_id={"sec": sector - 1}, device_id_type=MESH)
+
+    @pl.when(sector < last)
+    def _():
+        pl.semaphore_signal(barrier, inc=1, device_id={"sec": sector + 1}, device_id_type=MESH)
+
+    left_load.start()
+    right_load.start()
+    sides = (sector > 0).astype(jnp.int32) + (sector < last).astype(jnp.int32)
+    pl.semaphore_wait(barrier, len(peers) + sides)
+    own_load.wait()
+
+    sent = []
+
+    def pass_on(owner, target, send_sem, recv_sem):
+        copy = pltpu.make_async_remote_copy(
+            src_ref=state.at[owner],
+            dst_ref=state.at[owner],
+            send_sem=send_sem,
+            recv_sem=recv_sem,
+            device_id={"ops": target},
+            device_id_type=MESH,
+        )
+        copy.start()
+        sent.append(copy)
+
+    def arrive(owner, recv_sem):
+        pltpu.make_async_copy(state.at[owner], state.at[owner], recv_sem).wait()
+
+    def to_cross(k, owner):
+        for j in range(1, crosses):
+            pass_on(owner, index_of(line, cross_at(j), core), cross_send.at[k, j], cross_recv.at[k, j])
+
+    def to_core(k, j, owner):
+        pass_on(owner, index_of(line, cross, other), core_send.at[k, j], core_recv.at[k, j])
+
+    for k in sorted(range(1, lines), key=lambda k: -min(k, lines - k)):
+        pass_on(position, index_of(line_at(k), cross, core), line_send.at[k], line_recv.at[k])
+    to_cross(0, position)
+    to_core(0, 0, position)
+    near_first = sorted(range(1, lines), key=lambda k: min(k, lines - k))
+    for k in near_first:
+        owner = index_of(line_at(lines - k), cross, core)
+        arrive(owner, line_recv.at[k])
+        to_cross(k, owner)
+        to_core(k, 0, owner)
+    for k in [0] + near_first:
+        for j in range(1, crosses):
+            owner = index_of(line_at(lines - k), cross_at(crosses - j), core)
+            arrive(owner, cross_recv.at[k, j])
+            to_core(k, j, owner)
+    for k in [0] + near_first:
+        for j in range(crosses):
+            owner = index_of(line_at(lines - k), cross_at(crosses - j), other)
+            arrive(owner, core_recv.at[k, j])
+
+    @pl.when(sector > 0)
+    def _():
+        pl.semaphore_signal(ready_sem, inc=1, device_id={"sec": sector - 1}, device_id_type=MESH)
+
+    left_load.wait()
+    right_load.wait()
+
+    @pl.when(sector < last)
+    def _():
+        live_count = counts_ref[0, position]
+        far = lax.rem(line * CHUNKS // lines + 1, CHUNKS)
+
+        def partial(half, start):
+            stacked = left[:, pl.ds(start, per_chunk), half].reshape(slots * rows, columns)
+            whole = state[...].reshape(chips * CORES * band, columns)
+            products = jnp.dot(stacked, whole, preferred_element_type=jnp.float32)
+            total = None
+            for slot in range(slots):
+                live = (slot < live_count).astype(jnp.float32)
+                product = (products[slot * rows:(slot + 1) * rows] * live).astype(jnp.bfloat16)
+                term = jnp.dot(product, right[picks_ref[0, slot]], preferred_element_type=jnp.float32)
+                total = term if total is None else total + term
+            return total
+
+        starts = [lax.rem(far + n, CHUNKS) * per_chunk for n in range(CHUNKS)]
+        halves = []
+        for n in range(CHUNKS):
+            mine[n] = partial(other, starts[n])
+            copy = pltpu.make_async_remote_copy(
+                src_ref=mine.at[n],
+                dst_ref=theirs.at[n],
+                send_sem=half_send.at[n],
+                recv_sem=half_recv.at[n],
+                device_id={"ops": index_of(line, cross, other)},
+                device_id_type=MESH,
+            )
+            copy.start()
+            halves.append(copy)
+        pl.semaphore_wait(ready_sem, 1)
+        bands = []
+        for n in range(CHUNKS):
+            total = partial(core, starts[n])
+            halves[n].wait()
+            total = total + theirs[n]
+            banded[n] = total.reshape(per_chunk, band, columns).astype(jnp.bfloat16)
+            for m in range(per_chunk):
+                copy = pltpu.make_async_remote_copy(
+                    src_ref=banded.at[n, m],
+                    dst_ref=landed.at[chip],
+                    send_sem=band_send.at[n, m],
+                    recv_sem=band_recv.at[chip],
+                    device_id={"ops": (starts[n] + m) * CORES + core, "sec": sector + 1},
+                    device_id_type=MESH,
+                )
+                copy.start()
+                bands.append(copy)
+        for copy in bands:
+            copy.wait_send()
+
+    for copy in sent:
+        copy.wait_send()
+    onsite = 0.5 * charges_ref[0].astype(jnp.float32) * state[position].astype(jnp.float32)
+
+    @pl.when(sector == 0)
+    def _():
+        out_ref[...] = onsite.astype(out_ref.dtype)
+
+    @pl.when(sector > 0)
+    def _():
+        raised = jnp.zeros_like(onsite)
+        for source in range(chips):
+            pltpu.make_async_copy(landed.at[source], landed.at[source], band_recv.at[source]).wait()
+            raised = raised + landed[source].astype(jnp.float32)
+        out_ref[...] = (onsite + raised).astype(out_ref.dtype)
+
+
+def fused(wavefunction, left_blocks, right_blocks, pair_index, term_counts, charges):
+    devices = lax.axis_size("ops")
+    sectors = lax.axis_size("sec")
+    chips = devices // CORES
+    lines, crosses = line_lengths(chips)
+    _, band, columns = wavefunction.shape
+    slots = left_blocks.shape[1]
+    per_chunk = chips // CHUNKS
+    rows = per_chunk * band
+    bf16, f32 = jnp.bfloat16, jnp.float32
+    dma = pltpu.SemaphoreType.DMA
+    out = pl.pallas_call(
+        functools.partial(kernel, lines, crosses, sectors),
+        out_shape=jax.ShapeDtypeStruct((band, columns), wavefunction.dtype),
+        in_specs=[pl.BlockSpec(memory_space=pltpu.SMEM)] * 3 + [pl.BlockSpec(memory_space=pl.ANY)] * 3,
+        out_specs=pl.BlockSpec(memory_space=pltpu.VMEM),
+        scratch_shapes=[
+            pltpu.VMEM((devices, band, columns), bf16),
+            pltpu.VMEM((slots, chips, CORES, band, columns), bf16),
+            pltpu.VMEM((slots,) + right_blocks.shape[2:], bf16),
+            pltpu.VMEM((CHUNKS, rows, columns), f32),
+            pltpu.VMEM((CHUNKS, rows, columns), f32),
+            pltpu.VMEM((CHUNKS, per_chunk, band, columns), bf16),
+            pltpu.VMEM((chips, band, columns), bf16),
+            dma((3,)),
+            dma((lines,)),
+            dma((lines,)),
+            dma((lines, crosses)),
+            dma((lines, crosses)),
+            dma((lines, crosses)),
+            dma((lines, crosses)),
+            dma((CHUNKS,)),
+            dma((CHUNKS,)),
+            dma((CHUNKS, per_chunk)),
+            dma((chips,)),
+            pltpu.SemaphoreType.REGULAR,
+        ],
+        compiler_params=pltpu.CompilerParams(collective_id=0, has_side_effects=True),
+    )(
+        pair_index, term_counts, charges, wavefunction[0],
+        left_blocks[0].reshape(slots, chips, CORES, band, columns), right_blocks[0],
+    )
+    return out[None]
 
 
 def from_behind(x, axis, by):
@@ -23,20 +260,13 @@
     return lax.fori_loop(0, live_count, add_term, running)
 
 
-def per_device(wavefunction, left_blocks, right_blocks, pair_index, term_counts, charges):
+def unfused(wavefunction, left_blocks, right_blocks, pair_index, term_counts, charges):
     own_rows = wavefunction[0]
     gathered = lax.all_gather(own_rows, "ops", axis=0, tiled=True)
-    left_slots = left_blocks[0]
-    rights = right_blocks[0]
-    pair_picks = pair_index[0]
-    columns = gathered.shape[1]
-    position = lax.axis_index("ops")
-    counts_row = term_counts[0]
-    live_count = counts_row[position]
-    band_rows = own_rows.shape[0]
-    running = jnp.zeros((band_rows * lax.axis_size("ops"), columns), jnp.float32)
+    live_count = term_counts[0][lax.axis_index("ops")]
+    running = jnp.zeros(gathered.shape, jnp.float32)
     summed = lax.psum_scatter(
-        add_terms(running, gathered, left_slots, rights, pair_picks, live_count),
+        add_terms(running, gathered, left_blocks[0], right_blocks[0], pair_index[0], live_count),
         "ops",
         scatter_dimension=0,
         tiled=True,
@@ -44,6 +274,11 @@
     raised = from_behind(summed, "sec", 1)
     onsite = 0.5 * charges[0].astype(jnp.float32) * own_rows.astype(jnp.float32)
     return (onsite + raised).astype(jnp.bfloat16)[None]
+
+
+def per_device(wavefunction, *others):
+    aligned = wavefunction.shape[1] % ROW_TILE == 0 and lax.axis_size("ops") % (CORES * CHUNKS) == 0
+    return (fused if aligned else unfused)(wavefunction, *others)
 
 
 def solution(mesh):

time: 124 us -> 27.4 us (0.22)
  waiting for transfers between devices: 77.5 us -> 0 us
  Pallas kernels: 0 us -> 25.1 us
  blocking collectives: 24.9 us -> 0 us
  between operations: 14.1 us -> 0.66 us
  starting transfers between devices: 3.39 us -> 0 us
    reduce_scatter x1 -> x0, waiting for transfers between devices: 75.9 us -> none  [per_device(): lax.psum_scatter(add_terms(running, gathered, left_slots, rights, pair_pi...]
    pallas_call x0 -> x1, Pallas kernels: none -> 25.1 us  [fused(): pl.pallas_call(functools.partial(kernel, lines, crosses, sectors), out_sh...]
    all_gather x1 -> x0, blocking collectives: 24.9 us -> none  [per_device(): gathered = lax.all_gather(own_rows, 'ops', axis=0, tiled=True)]
    ppermute x1 -> x0, starting transfers between devices: 3.39 us -> none  [from_behind(): return lax.ppermute(x, axis, pairs)]
    ppermute x1 -> x0, waiting for transfers between devices: 1.55 us -> none  [from_behind(): return lax.ppermute(x, axis, pairs)]
  transfers between devices with their start and end apart: 2 -> 0, of which waited for: 2 -> 0; matrix products, arithmetic and copies ran while one was open for 0% -> 0% of each run, Pallas kernels for 0% -> 0%
where the time goes in v1:
time: 27.4 us; the launch traced here: 27.2 us
  Pallas kernels  25.1 us (92%)
  local copies, waits for them, and re-layouts  1.38 us (5%)
  between operations  0.66 us (2%)
    pallas_call x1, Pallas kernels, fused(): pl.pallas_call(functools.partial(kernel, lines, crosses, sectors), out_sh...  25.1 us
    unnamed x1, local copies, waits for them, and re-layouts  1.38 us

profile of v1, /device:TPU:0, one launch (start us, length us, event | category | flops | bytes accessed | tf_op | source)
XLA Modules:
  0.0 27.2 jit_solution(4661359088036634236)
XLA Ops:
  0.7 25.1 %shard_map.64 = bf16[32,512]{1,0:T(8,128)(2,1)} custom-call(s32[1,4]{1,0:T(1,128)} %picks_ref.1, s32[1,16]{1,0:T(1,128)} %counts_ref.1, s32[1]{0:T(128)S(6)} %copy.8.charges_ref, bf16[32,512]{1,0:T(8,128)(2,1)} %bitcast.7, bf16[4,8,2,32,512]{4,3,2,1,0:T(8,128)(2,1)} %bitcast.4, bf16[4,512,512]{2,1,0:T(8,128)(2,1)} %bitcast.5), custom_call_target="tpu_custom_call" | custom-call | tf_op jit(solution)/shard_map/pallas_call | solution.py:210
  25.8 1.4 %copy.9 = bf16[1,32,512]{2,1,0:T(8,128)(2,1)} copy(bf16[1,32,512]{2,1,0:T(8,128)(2,1)} %bitcast.6) | data formatting | bytes 65536

commit v2 on v1

--- a/solution.py
+++ b/solution.py
@@ -56,8 +56,7 @@
     right_load = pltpu.make_async_copy(right_hbm, right, load_sem.at[2])
 
     barrier = pltpu.get_barrier_semaphore()
-    peers = [index_of(line_at(k), cross, core) for k in range(1, lines)]
-    peers += [index_of(line, cross_at(k), core) for k in range(1, crosses)]
+    peers = [index_of(line_at(k), cross_at(j), core) for k in range(lines) for j in range(crosses) if k or j]
     peers += [index_of(line, cross, other)]
     for peer in peers:
         pl.semaphore_signal(barrier, inc=1, device_id={"ops": peer}, device_id_type=MESH)
@@ -93,32 +92,21 @@
     def arrive(owner, recv_sem):
         pltpu.make_async_copy(state.at[owner], state.at[owner], recv_sem).wait()
 
-    def to_cross(k, owner):
-        for j in range(1, crosses):
-            pass_on(owner, index_of(line, cross_at(j), core), cross_send.at[k, j], cross_recv.at[k, j])
-
     def to_core(k, j, owner):
         pass_on(owner, index_of(line, cross, other), core_send.at[k, j], core_recv.at[k, j])
 
-    for k in sorted(range(1, lines), key=lambda k: -min(k, lines - k)):
-        pass_on(position, index_of(line_at(k), cross, core), line_send.at[k], line_recv.at[k])
-    to_cross(0, position)
+    steps = [(k, j) for k in range(lines) for j in range(crosses)]
+    near = sorted(steps, key=lambda s: (min(s[0], lines - s[0]), s[1]))
+    for k, j in near[:0:-1]:
+        pass_on(position, index_of(line_at(k), cross_at(j), core), cross_send.at[k, j], cross_recv.at[k, j])
     to_core(0, 0, position)
-    near_first = sorted(range(1, lines), key=lambda k: min(k, lines - k))
-    for k in near_first:
-        owner = index_of(line_at(lines - k), cross, core)
-        arrive(owner, line_recv.at[k])
-        to_cross(k, owner)
-        to_core(k, 0, owner)
-    for k in [0] + near_first:
-        for j in range(1, crosses):
-            owner = index_of(line_at(lines - k), cross_at(crosses - j), core)
-            arrive(owner, cross_recv.at[k, j])
-            to_core(k, j, owner)
-    for k in [0] + near_first:
-        for j in range(crosses):
-            owner = index_of(line_at(lines - k), cross_at(crosses - j), other)
-            arrive(owner, core_recv.at[k, j])
+    for k, j in near[1:]:
+        owner = index_of(line_at(lines - k), cross_at(crosses - j), core)
+        arrive(owner, cross_recv.at[k, j])
+        to_core(k, j, owner)
+    for k, j in near:
+        owner = index_of(line_at(lines - k), cross_at(crosses - j), other)
+        arrive(owner, core_recv.at[k, j])
 
     @pl.when(sector > 0)
     def _():
@@ -209,7 +197,7 @@
     dma = pltpu.SemaphoreType.DMA
     out = pl.pallas_call(
         functools.partial(kernel, lines, crosses, sectors),
-        out_shape=jax.ShapeDtypeStruct((band, columns), wavefunction.dtype),
+        out_shape=pltpu.VMEM((band, columns), wavefunction.dtype),
         in_specs=[pl.BlockSpec(memory_space=pltpu.SMEM)] * 3 + [pl.BlockSpec(memory_space=pl.ANY)] * 3,
         out_specs=pl.BlockSpec(memory_space=pltpu.VMEM),
         scratch_shapes=[

time: 27.4 us -> 24.7 us (0.901)
  the two profiles are of different devices: /device:TPU:0 before, /device:TPU:15 now
where the time goes in v2:
time: 24.7 us; the launch traced here: 24.5 us
  Pallas kernels  23.2 us (94%)
  between operations  0.66 us (3%)
  local copies, waits for them, and re-layouts  0.62 us (3%)
    pallas_call x1, Pallas kernels, fused(): pl.pallas_call(functools.partial(kernel, lines, crosses, sectors), out_sh...  23.2 us
    unnamed x1, local copies, waits for them, and re-layouts  0.62 us

profile of v2, /device:TPU:15, one launch (start us, length us, event | category | flops | bytes accessed | tf_op | source)
XLA Modules:
  0.0 24.5 jit_solution(13489829883424450492)
XLA Ops:
  0.7 23.2 %shard_map.64 = bf16[32,512]{1,0:T(8,128)(2,1)S(1)} custom-call(s32[1,4]{1,0:T(1,128)} %picks_ref.1, s32[1,16]{1,0:T(1,128)} %counts_ref.1, s32[1]{0:T(128)S(6)} %copy.9.charges_ref, bf16[32,512]{1,0:T(8,128)(2,1)} %bitcast.7, bf16[4,8,2,32,512]{4,3,2,1,0:T(8,128)(2,1)} %bitcast.5, bf16[4,512,512]{2,1,0:T(8,128)(2,1)} %bitcast.6), custom_call_target="tpu_custom_call" | custom-call | tf_op jit(solution)/shard_map/pallas_call | solution.py:198
  23.9 0.6 %copy.8 = bf16[1,32,512]{2,1,0:T(8,128)(2,1)} copy(bf16[1,32,512]{2,1,0:T(8,128)(2,1)S(1)} %bitcast.4) | data formatting | bytes 65536

commit v3 on v2

--- a/solution.py
+++ b/solution.py
@@ -22,8 +22,9 @@
 
 def kernel(
     lines, crosses, sectors,
-    picks_ref, counts_ref, charges_ref, own_hbm, left_hbm, right_hbm,
+    picks_hbm, counts_hbm, charges_hbm, own_hbm, left_hbm, right_hbm,
     out_ref,
+    picks_ref, counts_ref, charges_ref,
     state, left, right, mine, theirs, banded, landed,
     load_sem, line_send, line_recv, cross_send, cross_recv, core_send, core_recv,
     half_send, half_recv, band_send, band_recv, ready_sem,
@@ -71,6 +72,13 @@
 
     left_load.start()
     right_load.start()
+    small_loads = [
+        pltpu.make_async_copy(picks_hbm, picks_ref, load_sem.at[3]),
+        pltpu.make_async_copy(counts_hbm, counts_ref, load_sem.at[4]),
+        pltpu.make_async_copy(charges_hbm, charges_ref, load_sem.at[5]),
+    ]
+    for load in small_loads:
+        load.start()
     sides = (sector > 0).astype(jnp.int32) + (sector < last).astype(jnp.int32)
     pl.semaphore_wait(barrier, len(peers) + sides)
     own_load.wait()
@@ -97,7 +105,8 @@
 
     steps = [(k, j) for k in range(lines) for j in range(crosses)]
     near = sorted(steps, key=lambda s: (min(s[0], lines - s[0]), s[1]))
-    for k, j in near[:0:-1]:
+
+    for k, j in sorted(near[1:], key=lambda s: (-min(s[0], lines - s[0]), -s[1])):
         pass_on(position, index_of(line_at(k), cross_at(j), core), cross_send.at[k, j], cross_recv.at[k, j])
     to_core(0, 0, position)
     for k, j in near[1:]:
@@ -114,6 +123,8 @@
 
     left_load.wait()
     right_load.wait()
+    for load in small_loads:
+        load.wait()
 
     @pl.when(sector < last)
     def _():
@@ -198,9 +209,12 @@
     out = pl.pallas_call(
         functools.partial(kernel, lines, crosses, sectors),
         out_shape=pltpu.VMEM((band, columns), wavefunction.dtype),
-        in_specs=[pl.BlockSpec(memory_space=pltpu.SMEM)] * 3 + [pl.BlockSpec(memory_space=pl.ANY)] * 3,
+        in_specs=[pl.BlockSpec(memory_space=pl.ANY)] * 6,
         out_specs=pl.BlockSpec(memory_space=pltpu.VMEM),
         scratch_shapes=[
+            pltpu.SMEM(pair_index.shape, pair_index.dtype),
+            pltpu.SMEM(term_counts.shape, term_counts.dtype),
+            pltpu.SMEM(charges.shape, charges.dtype),
             pltpu.VMEM((devices, band, columns), bf16),
             pltpu.VMEM((slots, chips, CORES, band, columns), bf16),
             pltpu.VMEM((slots,) + right_blocks.shape[2:], bf16),
@@ -208,7 +222,7 @@
             pltpu.VMEM((CHUNKS, rows, columns), f32),
             pltpu.VMEM((CHUNKS, per_chunk, band, columns), bf16),
             pltpu.VMEM((chips, band, columns), bf16),
-            dma((3,)),
+            dma((6,)),
             dma((lines,)),
             dma((lines,)),
             dma((lines, crosses)),

time: 24.7 us -> 24 us (0.972)
  Pallas kernels: 23.2 us -> 22.6 us
    pallas_call x1, Pallas kernels: 23.2 us -> 22.6 us  [fused(): pl.pallas_call(functools.partial(kernel, lines, crosses, sectors), out_sh...]
where the time goes in v3:
time: 24 us; the launch traced here: 23.8 us
  Pallas kernels  22.6 us (94%)
  between operations  0.66 us (3%)
  local copies, waits for them, and re-layouts  0.62 us (3%)
    pallas_call x1, Pallas kernels, fused(): pl.pallas_call(functools.partial(kernel, lines, crosses, sectors), out_sh...  22.6 us
    unnamed x1, local copies, waits for them, and re-layouts  0.62 us

profile of v3, /device:TPU:15, one launch (start us, length us, event | category | flops | bytes accessed | tf_op | source)
XLA Modules:
  0.0 23.8 jit_solution(15966732173215892158)
XLA Ops:
  0.7 22.6 %shard_map.64 = bf16[32,512]{1,0:T(8,128)(2,1)S(1)} custom-call(s32[1,4]{1,0:T(1,128)} %picks_hbm.1, s32[1,16]{1,0:T(1,128)} %counts_hbm.1, s32[1]{0:T(128)S(6)} %copy.9.charges_hbm, bf16[32,512]{1,0:T(8,128)(2,1)} %bitcast.7, bf16[4,8,2,32,512]{4,3,2,1,0:T(8,128)(2,1)} %bitcast.5, bf16[4,512,512]{2,1,0:T(8,128)(2,1)} %bitcast.6), custom_call_target="tpu_custom_call" | custom-call | tf_op jit(solution)/shard_map/pallas_call | solution.py:209
  23.2 0.6 %copy.8 = bf16[1,32,512]{2,1,0:T(8,128)(2,1)} copy(bf16[1,32,512]{2,1,0:T(8,128)(2,1)S(1)} %bitcast.4) | data formatting | bytes 65536
